TPU v7x, 256 devices: a whole 4x4x8 slice. The times are simulated.
256 devices in a mesh: param: 16 (over z, core), ex: 16 (over x, y).
Axes of the slice: x: 4, y: 4, z: 8, core: 2. Of those that a mesh axis runs over, the one named last changes fastest.
Arguments:
- query_acts: bfloat16 [16, 256, 16, 4096], P(None, 'ex', None, 'param'), may hold values from -6 to 6
- query_grads: bfloat16 [16, 256, 16, 4096], P(None, 'ex', None, 'param'), may hold values from -6 to 6
- train_acts: bfloat16 [16, 512, 16, 4096], P(None, 'ex', None, 'param'), as said below
- train_grads: bfloat16 [16, 512, 16, 4096], P(None, 'ex', None, 'param'), as said below
- input_projection: bfloat16 [4096, 128], P('param'), as said below
- proj_out: bfloat16 [4096, 64], P('param'), as said below
- query_clusters: int32 [16, 256], P('param'), may hold values from 0 to 127
- train_clusters: int32 [16, 512], P(None, 'ex'), may hold values from 0 to 127
- pair_mask: int32 [128, 128], replicated, may hold values 0 or 1
Outputs:
- scores: float32 [16, 256, 16, 512], P('param', None, None, 'ex')
- cluster_scores: float32 [16, 256, 128], P('param', 'ex')
Inputs may be any that keep to these rules, and one draw needn't show every extreme that they name: `train_acts`: token features whose scales differ from token to token and from example to example. `train_grads`: token gradients whose scales differ from example to example. `input_projection`: random projection columns of differing scales. `proj_out`: random projection columns of differing scales.
All inputs are finite; a program needn't handle non-finite values.
Results may differ from a plain program's by a relative error of at most 0.022.
The roundings to bfloat16 on the way count: a program that leaves them out, or rounds other values in their place, can miss the bound.
Values may be sent and summed in bfloat16 or wider, within the bound.
A program may use at most 128 MiB of HBM per device.

v0:
```python
import math
import jax
import jax.numpy as jnp
from jax import lax
from jax.sharding import PartitionSpec as P


def inverse_of(gram, count):
    mean = gram / count
    size = gram.shape[0]
    damping = 0.1 * jnp.trace(mean) / size
    identity = jnp.eye(size, dtype=gram.dtype)
    factor = jnp.linalg.cholesky(mean + damping * identity)
    return jax.scipy.linalg.cho_solve((factor, True), identity)


def form_grads(part_out, part_in):
    examples = part_out.shape[0]
    grad = jnp.einsum("tkr,tks->trs", part_out, part_in, preferred_element_type=jnp.float32)
    return grad.reshape(examples, -1).astype(jnp.bfloat16)


def shards(
    query_acts,
    query_grads,
    train_acts,
    train_grads,
    input_projection,
    proj_out,
    query_clusters,
    train_clusters,
    pair_mask,
):
    group_batches = train_acts.shape[0]
    query_rows = query_acts.shape[1]
    train_rows = train_acts.shape[1]
    tokens = train_acts.shape[2]
    width_in = input_projection.shape[1]
    width_out = proj_out.shape[1]
    clusters = pair_mask.shape[0]
    pieces = []
    for acts, grads in ((query_acts, query_grads), (train_acts, train_grads)):
        lead = acts.shape[:3]
        flat_acts = acts.reshape(-1, acts.shape[3])
        flat_grads = grads.reshape(-1, grads.shape[3])
        joined = jnp.concatenate(
            [
                jnp.dot(flat_acts, input_projection, preferred_element_type=jnp.float32),
                jnp.dot(flat_grads, proj_out, preferred_element_type=jnp.float32),
            ],
            axis=1,
        )
        pieces.append(joined.reshape(lead + (width_in + width_out,)))
    projected = lax.psum_scatter(
        jnp.concatenate(pieces, axis=1), "param", scatter_dimension=0, tiled=True
    ).astype(jnp.bfloat16)
    factors = projected[0]
    query_in = factors[:query_rows, :, :width_in]
    query_output_side = factors[:query_rows, :, width_in:]
    train_in = factors[query_rows:, :, :width_in]
    train_out = factors[query_rows:, :, width_in:]
    flat_in = train_in.reshape(-1, width_in)
    flat_out = train_out.reshape(-1, width_out)
    gram_in = jnp.dot(flat_in.T, flat_in, preferred_element_type=jnp.float32)
    gram_out = jnp.dot(flat_out.T, flat_out, preferred_element_type=jnp.float32)
    gram_in, gram_out = lax.psum((gram_in, gram_out), ("param", "ex"))
    total_train = group_batches * train_rows * lax.axis_size("ex")
    count = float(total_train * tokens)
    inv_in = inverse_of(gram_in, count)
    inv_out = inverse_of(gram_out, count)
    preconditioned_input = jnp.dot(
        query_in.reshape(-1, width_in).astype(jnp.float32), inv_in, precision=lax.Precision.HIGHEST
    ).reshape(query_rows, tokens, width_in)
    preconditioned_output = jnp.dot(
        query_output_side.reshape(-1, width_out).astype(jnp.float32),
        inv_out,
        precision=lax.Precision.HIGHEST,
    ).reshape(query_rows, tokens, width_out)
    query_before_preconditioning = jnp.einsum(
        "bui,bux->bix", preconditioned_output, preconditioned_input, precision=lax.Precision.HIGHEST
    )
    query_before_preconditioning = query_before_preconditioning.reshape(query_rows, -1).astype(
        jnp.bfloat16
    )
    trains = lax.all_gather(form_grads(train_out, train_in), "param", axis=0, tiled=True)
    cluster_ids = jnp.arange(clusters, dtype=jnp.int32)
    train_onehot = train_clusters.reshape(-1)[:, None] == cluster_ids[None, :]
    train_side = train_onehot.astype(jnp.bfloat16)
    mask_values = pair_mask.astype(jnp.bfloat16)
    scale = 1.0 / (tokens * math.sqrt(width_in * width_out))
    contract = (((1,), (1,)), ((), ()))
    ids = query_clusters[0]
    query_onehot = (ids[:, None] == cluster_ids[None, :]).astype(jnp.bfloat16)
    picked = jnp.dot(query_onehot, mask_values, preferred_element_type=jnp.float32).astype(
        jnp.bfloat16
    )
    allowed = lax.dot_general(picked, train_side, contract, preferred_element_type=jnp.float32)
    raw = lax.dot_general(
        lax.all_gather(query_before_preconditioning, "ex", axis=0, tiled=True),
        trains,
        contract,
        preferred_element_type=jnp.float32,
    )
    scores = raw * scale * allowed
    partial_value = jnp.dot(
        scores, train_onehot.astype(jnp.float32), precision=lax.Precision.HIGHEST
    ) * math.sqrt(clusters / total_train)
    summed = lax.psum_scatter(
        partial_value.astype(jnp.bfloat16), "ex", scatter_dimension=0, tiled=True
    ).astype(jnp.float32)
    all_queries = scores.shape[0]
    return (
        scores.reshape(1, all_queries, group_batches, train_rows),
        summed.reshape(1, summed.shape[0], clusters),
    )


def solution(mesh):
    return jax.shard_map(
        shards,
        mesh=mesh,
        in_specs=(
            P(None, "ex", None, "param"),
            P(None, "ex", None, "param"),
            P(None, "ex", None, "param"),
            P(None, "ex", None, "param"),
            P("param", None),
            P("param", None),
            P("param", None),
            P(None, "ex"),
            P(),
        ),
        out_specs=(P("param", None, None, "ex"), P("param", "ex", None)),
        check_vma=False,
    )
```

profile of v0, /device:TPU:2, one launch (start us, length us, event | category | flops | bytes accessed | tf_op | source)
XLA Modules:
  0.0 642.3 jit_solution(12987489176357474776)
XLA Ops:
  7.2 3.8 fusion.27
  11.1 1.4 fusion.28
  12.5 3.1 pad_maximum_fusion.1
  15.6 8.4 %copy.28 = f32[8192,192]{1,0:T(8,128)} copy(f32[8192,192]{0,1:T(8,128)} %pad_maximum_fusion.1) | data formatting | bytes 12582912 | tf_op jit(solution)/shard_map/concatenate | solution.py:46
  24.1 13.1 %copy.30 = f32[16,32,16,192]{3,1,2,0:T(8,128)} copy(f32[16,32,16,192]{3,2,1,0:T(8,128)} %bitcast.70) | data formatting | bytes 12582912 | tf_op jit(solution)/shard_map/reshape | solution.py:53
  37.2 0.8 fusion.25
  38.0 0.8 copy-done.3
  38.7 0.7 fusion.26
  39.5 2.0 pad_maximum_fusion.2
  41.4 5.1 copy.27
  46.6 7.4 %copy.29 = f32[16,16,16,192]{3,1,2,0:T(8,128)} copy(f32[16,16,16,192]{3,2,1,0:T(8,128)} %bitcast.71) | data formatting | bytes 6291456 | tf_op jit(solution)/shard_map/reshape | solution.py:53
  54.0 11.0 %pad_maximum_fusion = f32[16,48,16,192]{3,1,2,0:T(8,128)} fusion(f32[16,32,16,192]{3,1,2,0:T(8,128)} %copy.30, f32[16,16,16,192]{3,1,2,0:T(8,128)} %copy.29), kind=kLoop, calls=%fused_computation | loop fusion | flops 2359296 | bytes 18874368 | tf_op jit(solution)/shard_map/concatenate | solution.py:55
  65.1 82.4 %reduce-scatter.2.cloned.1.call-done = f32[1,48,16,192]{3,1,2,0:T(8,128)} async-done(((f32[16,48,16,192]{3,1,2,0:T(8,128)}), f32[1,48,16,192]{3,1,2,0:T(8,128)}) %reduce-scatter.2.cloned.1.call-update) | async-done | bytes 589840 | tf_op jit(solution)/shard_map/reduce_scatter | solution.py:54
  147.4 1.2 convert_bitcast_fusion
  148.6 0.9 convolution_bitcast_fusion.1
  149.5 0.2 convolution_bitcast_fusion.3
  149.8 75.2 %psum.14 = f32[64,64]{1,0:T(8,128)S(1)} all-reduce(f32[64,64]{1,0:T(8,128)S(1)} %convolution_bitcast_fusion.3), channel_id=1, replica_groups=mesh['param'=16,'ex'=16] {'param','ex'}, use_global_device_ids=true, to_apply=%region_1.0 | all-reduce | flops 4096 | bytes 32768 | tf_op jit(solution)/shard_map/psum | solution.py:66
  225.0 0.6 select_reduce_fusion.3
  226.4 5.8 cholesky.33
  232.3 0.6 compare_reduce_fusion.1
  232.9 0.7 fusion.16
  233.6 4.9 custom-call.20
  238.5 0.2 fusion.18
  239.1 155.0 %all-reduce.4.cloned.1.call-done = f32[128,128]{1,0:T(8,128)} async-done(((f32[128,128]{1,0:T(8,128)}), f32[128,128]{1,0:T(8,128)}) %all-reduce.4.cloned.1.call-update) | async-done | bytes 65552 | tf_op jit(solution)/shard_map/psum | solution.py:66
  394.1 1.5 select_reduce_fusion.1
  396.3 0.9 select_add_fusion
  397.2 0.9 fusion.9
  398.1 11.7 %cholesky.68 = f32[128,128]{1,0:T(8,128)S(1)} custom-call(f32[128,128]{1,0:T(8,128)S(1)} %fusion.9), custom_call_target="Cholesky" | custom-call | tf_op jit(solution)/shard_map/jit(cholesky)/cholesky | solution.py:13
  409.8 0.6 compare_reduce_fusion
  410.5 0.7 fusion.5
  411.1 9.8 %custom-call.21 = f32[1,128,128]{1,2,0:T(8,128)S(1)} custom-call(f32[1,128,128]{2,1,0:T(8,128)S(1)} %fusion.5), custom_call_target="InvertDiagBlocksLowerTriangular" | custom-call | tf_op jit(solution)/shard_map/jit(_cho_solve)/triangular_solve | solution.py:14
  420.9 0.2 fusion.7
  421.2 0.2 convolution_bitcast_fusion
  421.4 0.2 fusion.10
  421.6 1.0 convolution_convert_fusion.1
  422.6 0.9 copy.51
  423.7 0.3 convolution_convert_fusion
  424.0 1.1 copy.50
  425.2 0.3 all-reduce.6.cloned.1.call-start
  425.5 51.9 %all-gather.3.cloned.1.call-done = bf16[256,8192]{1,0:T(8,128)(2,1)} async-done(((bf16[16,8192]{1,0:T(8,128)(2,1)}), bf16[256,8192]{1,0:T(8,128)(2,1)}) %all-gather.3.cloned.1.call-update) | async-done | bytes 4194320 | tf_op jit(solution)/shard_map/all_gather | solution.py:99
  477.5 57.9 %all-gather.5.cloned.1.call-done = bf16[512,8192]{1,0:T(8,128)(2,1)} async-done(((bf16[32,8192]{1,0:T(8,128)(2,1)}), bf16[512,8192]{1,0:T(8,128)(2,1)}) %all-gather.5.cloned.1.call-update) | async-done | bytes 8388624 | tf_op jit(solution)/shard_map/all_gather | solution.py:85
  535.3 7.2 %convolution_multiply_fusion.1 = f32[256,512]{1,0:T(8,128)S(1)} fusion(bf16[256,8192]{1,0:T(8,128)(2,1)} %all-gather.3.cloned.1.call-done, bf16[512,8192]{1,0:T(8,128)(2,1)} %all-gather.5.cloned.1.call-done), kind=kOutput, calls=%fused_computation.5 | convolution fusion | flops 2147614720 | bytes 13107200 | tf_op jit(solution)/shard_map/dot_general | solution.py:98
  542.5 0.4 convolution_multiply_fusion
  542.9 1.1 fusion
  544.1 0.6 dynamic-slice
  545.3 1.0 copy.37
  546.3 88.2 %all-reduce.6.cloned.1.call-done = bf16[256,128]{1,0:T(8,128)(2,1)} async-done(((bf16[256,128]{1,0:T(8,128)(2,1)}), bf16[256,128]{1,0:T(8,128)(2,1)}) %all-reduce.6.cloned.1.call-update) | async-done | bytes 65552
  634.5 1.3 bitcast_convert_fusion
  (41 shorter events, 1.1 us)
Async XLA Ops:
  7.2 30.0 %copy-start = (bf16[16,16,16,256]{3,2,1,0:T(8,128)(2,1)S(1)}, bf16[16,16,16,256]{3,2,1,0:T(8,128)(2,1)}, u32[]{:S(2)}) copy-start(bf16[16,16,16,256]{3,2,1,0:T(8,128)(2,1)} %param.9) | copy-start | bytes 6291460
  7.2 140.3 %reduce-scatter.2.cloned.1.call-start = ((), (), s32[]{:S(2)}) async-start(), calls=%async_computation.1 | async-start | bytes 13369344 | tf_op jit(solution)/shard_map/reduce_scatter | solution.py:54
  7.2 3.9 copy-start.2
  7.2 3.9 copy-start.5
  24.1 13.1 %copy-start.4 = (bf16[256,128]{1,0:T(8,128)(2,1)S(1)}, bf16[256,128]{1,0:T(8,128)(2,1)}, u32[]{:S(2)}) copy-start(bf16[256,128]{1,0:T(8,128)(2,1)} %param.13) | copy-start | bytes 196612
  37.1 1.6 copy-start.3
  65.0 360.5 %copy-start.7 = (s32[16,32]{1,0:T(8,128)S(1)}, s32[16,32]{1,0:T(8,128)}, u32[]{:S(2)}) copy-start(s32[16,32]{1,0:T(8,128)} %param.16) | copy-start | bytes 6148
  65.0 329.1 %all-reduce.4.cloned.1.call-start = ((), (), s32[]{:S(2)}) async-start(), calls=%async_computation.2 | async-start | bytes 131072 | tf_op jit(solution)/shard_map/psum | solution.py:66
  149.7 327.7 %all-gather.3.cloned.1.call-start = ((), (), s32[]{:S(2)}) async-start(), calls=%async_computation.3 | async-start | bytes 4456448 | tf_op jit(solution)/shard_map/all_gather | solution.py:99
  423.6 111.8 %all-gather.5.cloned.1.call-start = ((), (), s32[]{:S(2)}) async-start(), calls=%async_computation.4 | async-start | bytes 8912896 | tf_op jit(solution)/shard_map/all_gather | solution.py:85
  425.2 209.3 %all-reduce.6.cloned.1.call-start = ((), (), s32[]{:S(2)}) async-start(), calls=%async_computation.5 | async-start | bytes 131072
  425.5 117.0 %copy-start.6 = (s32[128,128]{1,0:T(8,128)S(1)}, s32[128,128]{1,0:T(8,128)}, u32[]{:S(2)}) copy-start(s32[128,128]{1,0:T(8,128)} %param.17) | copy-start | bytes 196612
  425.5 117.0 %copy-start.8 = (s32[1,256]{1,0:T(1,128)S(1)}, s32[1,256]{1,0:T(1,128)}, u32[]{:S(2)}) copy-start(s32[1,256]{1,0:T(1,128)} %param.15) | copy-start | bytes 3076
  425.5 118.5 %copy-start.9 = (u32[256]{0:T(256)S(1)}, u32[256]{0:T(256)}, u32[]{:S(2)}) copy-start(u32[256]{0:T(256)} %constant.124) | copy-start | bytes 3076
  535.3 100.4 %copy-start.1 = (bf16[16,16,16,256]{3,2,1,0:T(8,128)(2,1)S(1)}, bf16[16,16,16,256]{3,2,1,0:T(8,128)(2,1)}, u32[]{:S(2)}) copy-start(bf16[16,16,16,256]{3,2,1,0:T(8,128)(2,1)} %param.9) | copy-start | bytes 6291460
Sparse Core Ops, SparseCore 0:
  65.1 82.2 reduce-scatter.1
  153.5 240.5 all-reduce.3
  423.7 53.7 all-gather.2
  479.7 55.5 all-gather.4
  544.2 90.2 all-reduce.5
where the time goes:
time: 643 us; the launch traced here: 642 us
  waiting for transfers between devices  436 us (68%)
  blocking collectives  75.2 us (12%)
  other arithmetic  57.3 us (9%)
  local copies, waits for them, and re-layouts  38.8 us (6%)
  matrix products  19.1 us (3%)
  between operations  16 us (2%)
    psum x1, waiting for transfers between devices, shards(): gram_in, gram_out = lax.psum((gram_in, gram_out), ('param', 'ex'))  155 us
    unnamed x6, waiting for transfers between devices  88.3 us
    reduce_scatter x1, waiting for transfers between devices, shards(): lax.psum_scatter(jnp.concatenate(pieces, axis=1), 'param', scatter_dimens...  82.4 us
    psum x1, blocking collectives, shards(): gram_in, gram_out = lax.psum((gram_in, gram_out), ('param', 'ex'))  75.2 us
    all_gather x1, waiting for transfers between devices, shards(): lax.all_gather(form_grads(train_out, train_in), 'param', axis=0, tiled=True)  57.9 us
    all_gather x1, waiting for transfers between devices, shards(): lax.all_gather(query_before_preconditioning, 'ex', axis=0, tiled=True)  51.9 us
    reshape x2, local copies, waits for them, and re-layouts, shards(): pieces.append(joined.reshape(lead + (width_in + width_out,)))  20.5 us
    another operation x6, other arithmetic, inverse_of(): factor = jnp.linalg.cholesky(mean + damping * identity)  18.9 us
  transfers between devices with their start and end apart: 5, of which 5 were waited for; matrix products, arithmetic and copies ran while one was open for 3% of the time, Pallas kernels for 0%

commit v1 on v0

--- a/solution.py
+++ b/solution.py
@@ -82,7 +82,11 @@
     query_before_preconditioning = query_before_preconditioning.reshape(query_rows, -1).astype(
         jnp.bfloat16
     )
-    trains = lax.all_gather(form_grads(train_out, train_in), "param", axis=0, tiled=True)
+    part = form_grads(train_out, train_in)
+    devices = lax.axis_size("param")
+    blocks = jnp.stack([part for _ in range(devices)])
+    blocks = lax.all_to_all(blocks, "param", split_axis=0, concat_axis=0)
+    trains = jnp.concatenate(blocks, axis=0)
     cluster_ids = jnp.arange(clusters, dtype=jnp.int32)
     train_onehot = train_clusters.reshape(-1)[:, None] == cluster_ids[None, :]
     train_side = train_onehot.astype(jnp.bfloat16)

time: 643 us -> 676 us (1.051)
  blocking collectives: 75.2 us -> 228 us
  waiting for transfers between devices: 436 us -> 307 us
    psum x1, blocking collectives: 75.2 us -> 228 us  [shards(): gram_in, gram_out = lax.psum((gram_in, gram_out), ('param', 'ex'))]
    psum x1, waiting for transfers between devices: 155 us -> 81.3 us  [shards(): gram_in, gram_out = lax.psum((gram_in, gram_out), ('param', 'ex'))]
    all_gather x1 -> x0, waiting for transfers between devices: 57.9 us -> none  [shards(): lax.all_gather(form_grads(train_out, train_in), 'param', axis=0, tiled=True)]
    unnamed x6 -> x5, waiting for transfers between devices: 88.3 us -> 89.4 us
  transfers between devices with their start and end apart: 5 -> 5, of which waited for: 5 -> 4; matrix products, arithmetic and copies ran while one was open for 3% -> 7% of each run, Pallas kernels for 0% -> 0%
where the time goes in v1:
time: 676 us; the launch traced here: 675 us
  waiting for transfers between devices  307 us (45%)
  blocking collectives  228 us (34%)
  other arithmetic  57.3 us (8%)
  local copies, waits for them, and re-layouts  42.2 us (6%)
  matrix products  19.1 us (3%)
  between operations  16 us (2%)
    psum x1, blocking collectives, shards(): gram_in, gram_out = lax.psum((gram_in, gram_out), ('param', 'ex'))  228 us
    unnamed x5, waiting for transfers between devices  89.4 us
    reduce_scatter x1, waiting for transfers between devices, shards(): lax.psum_scatter(jnp.concatenate(pieces, axis=1), 'param', scatter_dimens...  82.4 us
    psum x1, waiting for transfers between devices, shards(): gram_in, gram_out = lax.psum((gram_in, gram_out), ('param', 'ex'))  81.3 us
    all_gather x1, waiting for transfers between devices, shards(): lax.all_gather(query_before_preconditioning, 'ex', axis=0, tiled=True)  53.5 us
    reshape x2, local copies, waits for them, and re-layouts, shards(): pieces.append(joined.reshape(lead + (width_in + width_out,)))  20.5 us
    another operation x6, other arithmetic, inverse_of(): factor = jnp.linalg.cholesky(mean + damping * identity)  18.9 us
    another operation x4, other arithmetic, inverse_of(): return jax.scipy.linalg.cho_solve((factor, True), identity)  16 us
  transfers between devices with their start and end apart: 5, of which 4 were waited for; matrix products, arithmetic and copies ran while one was open for 7% of the time, Pallas kernels for 0%

profile of v1, /device:TPU:2, one launch (start us, length us, event | category | flops | bytes accessed | tf_op | source)
XLA Modules:
  0.0 675.4 jit_solution(18384120362491994865)
XLA Ops:
  7.2 3.8 fusion.27
  11.1 1.4 fusion.28
  12.5 3.1 pad_maximum_fusion.1
  15.6 8.4 %copy.28 = f32[8192,192]{1,0:T(8,128)} copy(f32[8192,192]{0,1:T(8,128)} %pad_maximum_fusion.1) | data formatting | bytes 12582912 | tf_op jit(solution)/shard_map/concatenate | solution.py:46
  24.1 13.1 %copy.30 = f32[16,32,16,192]{3,1,2,0:T(8,128)} copy(f32[16,32,16,192]{3,2,1,0:T(8,128)} %bitcast.71) | data formatting | bytes 12582912 | tf_op jit(solution)/shard_map/reshape | solution.py:53
  37.2 0.8 fusion.25
  38.0 0.8 copy-done.3
  38.7 0.7 fusion.26
  39.5 2.0 pad_maximum_fusion.2
  41.4 5.1 copy.27
  46.6 7.4 %copy.29 = f32[16,16,16,192]{3,1,2,0:T(8,128)} copy(f32[16,16,16,192]{3,2,1,0:T(8,128)} %bitcast.72) | data formatting | bytes 6291456 | tf_op jit(solution)/shard_map/reshape | solution.py:53
  54.0 11.0 %pad_maximum_fusion = f32[16,48,16,192]{3,1,2,0:T(8,128)} fusion(f32[16,32,16,192]{3,1,2,0:T(8,128)} %copy.30, f32[16,16,16,192]{3,1,2,0:T(8,128)} %copy.29), kind=kLoop, calls=%fused_computation | loop fusion | flops 2359296 | bytes 18874368 | tf_op jit(solution)/shard_map/concatenate | solution.py:55
  65.0 82.4 %reduce-scatter.2.cloned.1.call-done = f32[1,48,16,192]{3,1,2,0:T(8,128)} async-done(((f32[16,48,16,192]{3,1,2,0:T(8,128)}), f32[1,48,16,192]{3,1,2,0:T(8,128)}) %reduce-scatter.2.cloned.1.call-update) | async-done | bytes 589840 | tf_op jit(solution)/shard_map/reduce_scatter | solution.py:54
  147.4 1.2 convert_bitcast_fusion
  148.7 0.3 convolution_convert_fusion
  149.0 0.3 copy.50
  149.4 4.2 stack.2
  153.6 5.5 all-to-all-start
  159.2 0.9 convolution_bitcast_fusion.1
  160.4 228.2 %psum.14 = f32[64,64]{1,0:T(8,128)S(1)} all-reduce(f32[64,64]{1,0:T(8,128)S(1)} %convolution_bitcast_fusion.3), channel_id=1, replica_groups=mesh['param'=16,'ex'=16] {'param','ex'}, use_global_device_ids=true, to_apply=%region_1.0 | all-reduce | flops 4096 | bytes 32768 | tf_op jit(solution)/shard_map/psum | solution.py:66
  388.6 0.6 select_reduce_fusion.3
  390.0 5.8 cholesky.33
  395.8 0.6 compare_reduce_fusion.1
  396.5 0.7 fusion.16
  397.1 4.9 custom-call.20
  402.0 0.2 fusion.18
  402.7 81.3 %all-reduce.4.cloned.1.call-done = f32[128,128]{1,0:T(8,128)} async-done(((f32[128,128]{1,0:T(8,128)}), f32[128,128]{1,0:T(8,128)}) %all-reduce.4.cloned.1.call-update) | async-done | bytes 65552 | tf_op jit(solution)/shard_map/psum | solution.py:66
  483.9 1.5 select_reduce_fusion.1
  486.1 0.9 select_add_fusion
  487.0 0.9 fusion.9
  487.9 11.7 %cholesky.68 = f32[128,128]{1,0:T(8,128)S(1)} custom-call(f32[128,128]{1,0:T(8,128)S(1)} %fusion.9), custom_call_target="Cholesky" | custom-call | tf_op jit(solution)/shard_map/jit(cholesky)/cholesky | solution.py:13
  499.6 0.6 compare_reduce_fusion
  500.3 0.7 fusion.5
  500.9 9.8 %custom-call.21 = f32[1,128,128]{1,2,0:T(8,128)S(1)} custom-call(f32[1,128,128]{2,1,0:T(8,128)S(1)} %fusion.5), custom_call_target="InvertDiagBlocksLowerTriangular" | custom-call | tf_op jit(solution)/shard_map/jit(_cho_solve)/triangular_solve | solution.py:14
  510.8 0.2 fusion.7
  511.0 0.2 convolution_bitcast_fusion
  511.2 0.2 fusion.10
  511.4 1.0 convolution_convert_fusion.1
  512.5 0.9 copy.51
  513.4 0.3 all-reduce.6.cloned.1.call-start
  513.8 53.5 %all-gather.2.cloned.1.call-done = bf16[256,8192]{1,0:T(8,128)(2,1)} async-done(((bf16[16,8192]{1,0:T(8,128)(2,1)}), bf16[256,8192]{1,0:T(8,128)(2,1)}) %all-gather.2.cloned.1.call-update) | async-done | bytes 4194320 | tf_op jit(solution)/shard_map/all_gather | solution.py:103
  567.3 7.2 %convolution_multiply_fusion.1 = f32[256,512]{1,0:T(8,128)S(1)} fusion(bf16[256,8192]{1,0:T(8,128)(2,1)} %all-gather.2.cloned.1.call-done, bf16[512,8192]{1,0:T(8,128)(2,1)} %bitcast.17), kind=kOutput, calls=%fused_computation.5 | convolution fusion | flops 2147614720 | bytes 13107200 | tf_op jit(solution)/shard_map/dot_general | solution.py:102
  574.5 0.4 convolution_multiply_fusion
  574.9 1.1 fusion
  576.0 0.6 dynamic-slice
  577.3 1.0 copy.37
  578.3 89.4 %all-reduce.6.cloned.1.call-done = bf16[256,128]{1,0:T(8,128)(2,1)} async-done(((bf16[256,128]{1,0:T(8,128)(2,1)}), bf16[256,128]{1,0:T(8,128)(2,1)}) %all-reduce.6.cloned.1.call-update) | async-done | bytes 65552
  667.6 1.3 bitcast_convert_fusion
  (41 shorter events, 1.2 us)
Async XLA Ops:
  7.2 30.0 %copy-start = (bf16[16,16,16,256]{3,2,1,0:T(8,128)(2,1)S(1)}, bf16[16,16,16,256]{3,2,1,0:T(8,128)(2,1)}, u32[]{:S(2)}) copy-start(bf16[16,16,16,256]{3,2,1,0:T(8,128)(2,1)} %param.9) | copy-start | bytes 6291460
  7.2 140.3 %reduce-scatter.2.cloned.1.call-start = ((), (), s32[]{:S(2)}) async-start(), calls=%async_computation.2 | async-start | bytes 13369344 | tf_op jit(solution)/shard_map/reduce_scatter | solution.py:54
  7.2 3.9 copy-start.2
  7.2 3.9 copy-start.5
  24.1 13.1 %copy-start.4 = (bf16[256,128]{1,0:T(8,128)(2,1)S(1)}, bf16[256,128]{1,0:T(8,128)(2,1)}, u32[]{:S(2)}) copy-start(bf16[256,128]{1,0:T(8,128)(2,1)} %param.13) | copy-start | bytes 196612
  37.1 1.6 copy-start.3
  153.6 413.6 %all-to-all-start = ((bf16[16,32,8192]{2,1,0:T(8,128)(2,1)}), bf16[16,32,8192]{2,1,0:T(8,128)(2,1)}, u32[]{:S(2)}, u32[]{:S(2)}) async-start(bf16[16,32,8192]{2,1,0:T(8,128)(2,1)} %stack.2), calls=%async_computation.1 | async-start | bytes 16777216 | tf_op jit(solution)/shard_map/all_to_all | solution.py:88
  159.1 354.5 %copy-start.7 = (s32[16,32]{1,0:T(8,128)S(1)}, s32[16,32]{1,0:T(8,128)}, u32[]{:S(2)}) copy-start(s32[16,32]{1,0:T(8,128)} %param.16) | copy-start | bytes 6148
  159.1 324.8 %all-reduce.4.cloned.1.call-start = ((), (), s32[]{:S(2)}) async-start(), calls=%async_computation.3 | async-start | bytes 131072 | tf_op jit(solution)/shard_map/psum | solution.py:66
  160.1 407.2 %all-gather.2.cloned.1.call-start = ((), (), s32[]{:S(2)}) async-start(), calls=%async_computation.4 | async-start | bytes 4456448 | tf_op jit(solution)/shard_map/all_gather | solution.py:103
  513.4 154.3 %all-reduce.6.cloned.1.call-start = ((), (), s32[]{:S(2)}) async-start(), calls=%async_computation.5 | async-start | bytes 131072
  567.3 7.2 %copy-start.6 = (s32[128,128]{1,0:T(8,128)S(1)}, s32[128,128]{1,0:T(8,128)}, u32[]{:S(2)}) copy-start(s32[128,128]{1,0:T(8,128)} %param.17) | copy-start | bytes 196612
  567.3 7.2 %copy-start.8 = (s32[1,256]{1,0:T(1,128)S(1)}, s32[1,256]{1,0:T(1,128)}, u32[]{:S(2)}) copy-start(s32[1,256]{1,0:T(1,128)} %param.15) | copy-start | bytes 3076
  567.3 8.7 %copy-start.9 = (u32[256]{0:T(256)S(1)}, u32[256]{0:T(256)}, u32[]{:S(2)}) copy-start(u32[256]{0:T(256)} %constant.124) | copy-start | bytes 3076
  567.3 101.6 %copy-start.1 = (bf16[16,16,16,256]{3,2,1,0:T(8,128)(2,1)S(1)}, bf16[16,16,16,256]{3,2,1,0:T(8,128)(2,1)}, u32[]{:S(2)}) copy-start(bf16[16,16,16,256]{3,2,1,0:T(8,128)(2,1)} %param.9) | copy-start | bytes 6291460
Sparse Core Ops, SparseCore 0:
  65.1 82.2 reduce-scatter.1
  166.0 317.8 all-reduce.3
  513.5 53.7 all-gather.1
  576.1 91.4 all-reduce.5
